TPU v7x, 32 devices: a whole 2x2x4 slice. The times are simulated.
32 devices in a mesh: rep: 4 (over y, x), shard: 8 (over z, core).
Axes of the slice: x: 2, y: 2, z: 4, core: 2. Of those that a mesh axis runs over, the one named last changes fastest.
Arguments:
- block_in: bfloat16 [16384, 768], P(('rep', 'shard')), may hold values from -6 to 6
- earlier: bfloat16 [4, 16384, 768], P(None, ('rep', 'shard')), may hold values from -6 to 6
- cotangent: float32 [16384, 768], P(('rep', 'shard')), may hold values from -6 to 6
- qkv_weight: float32 [768, 2304], P('shard'), may hold values from -0.21875 to 0.21875
- out_weight: float32 [768, 768], P('shard'), may hold values from -6 to 6
- in_weight: float32 [768, 3072], P('shard'), may hold values from -0.21875 to 0.21875
- down_weight: float32 [3072, 768], P('shard'), may hold values from -0.109375 to 0.109375
- qk_bias: float32 [1536], P('shard'), may hold values from -3 to 3
- value_bias: float32 [768], P('shard'), may hold values from -3 to 3
- out_bias: float32 [768], P('shard'), may hold values from -3 to 3
- in_bias: float32 [3072], P('shard'), may hold values from -3 to 3
- down_bias: float32 [768], P('shard'), may hold values from -3 to 3
- gain_one: float32 [768], P('shard'), may hold values from 0.5 to 1.5
- shift_one: float32 [768], P('shard'), may hold values from -3 to 3
- gain_two: float32 [768], P('shard'), may hold values from 0.5 to 1.5
- shift_two: float32 [768], P('shard'), may hold values from -3 to 3
- depth_weights: float32 [5], replicated, may hold values from 0.3 to 1.2
Outputs:
- layer_out: float32 [16384, 768], P(('rep', 'shard'))
- grad_block_in: float32 [16384, 768], P(('rep', 'shard'))
- grad_earlier: float32 [4, 16384, 768], P(None, ('rep', 'shard'))
- grad_qkv_weight: float32 [768, 2304], P('shard')
- grad_out_weight: float32 [768, 768], P('shard')
- grad_in_weight: float32 [768, 3072], P('shard')
- grad_down_weight: float32 [3072, 768], P('shard')
- grad_qk_bias: float32 [1536], P('shard')
- grad_value_bias: float32 [768], P('shard')
- grad_out_bias: float32 [768], P('shard')
- grad_in_bias: float32 [3072], P('shard')
- grad_down_bias: float32 [768], P('shard')
- grad_gain_one: float32 [768], P('shard')
- grad_shift_one: float32 [768], P('shard')
- grad_gain_two: float32 [768], P('shard')
- grad_shift_two: float32 [768], P('shard')
- grad_depth: float32 [5], replicated
All inputs are finite; a program needn't handle non-finite values.
Results may differ from a plain program's by a relative error of at most 0.035.
Values may be sent and summed in bfloat16 or wider, within the bound.
No kernel may reach another device: no remote copies, remote signals or barrier semaphores. Data moves between devices by JAX's collectives and lax.ppermute only.
A program may use at most 192 MiB of HBM per device.

v0:
```python
from functools import partial
import math

import jax
import jax.numpy as jnp
from jax import lax
from jax.sharding import PartitionSpec as P

HEAD_DIM = 64
BLOCK = 256


NEG = -1e30
EPSILON = 1e-05


def layer_norm(inputs, gain, shift):
    center = inputs - jnp.mean(inputs, axis=-1, keepdims=True)
    spread = jnp.mean(center * center, axis=-1, keepdims=True)
    return center * lax.rsqrt(spread + EPSILON) * gain + shift


def rotate(inputs, positions):
    row_count = inputs.shape[0]
    split = inputs.reshape(row_count, -1, HEAD_DIM)
    half_dim = HEAD_DIM // 2
    freqs = 10000.0 ** (-jnp.arange(half_dim, dtype=jnp.float32) / half_dim)
    angles = positions.astype(jnp.float32)[:, None] * freqs[None, :]
    cosine = jnp.cos(angles)[:, None, :]
    sine = jnp.sin(angles)[:, None, :]
    former = split[..., :half_dim]
    latter = split[..., half_dim:]
    turned = jnp.concatenate(
        [former * cosine - latter * sine, former * sine + latter * cosine], axis=-1
    )
    return turned.reshape(row_count, -1)


def per_device(
    block_in,
    earlier,
    cotangent,
    qkv_weight,
    out_weight,
    in_weight,
    down_weight,
    qk_bias,
    value_bias,
    out_bias,
    in_bias,
    down_bias,
    gain_one,
    shift_one,
    gain_two,
    shift_two,
    depth_weights,
):
    bf16 = jnp.bfloat16
    f32 = jnp.float32
    w_qkv, w_out, w_in, w_down, b_qk, b_value, b_out, b_in, b_down, g_one, s_one, g_two, s_two = (
        lax.all_gather(qkv_weight.astype(bf16), "shard", axis=0, tiled=True),
        lax.all_gather(out_weight.astype(bf16), "shard", axis=0, tiled=True),
        lax.all_gather(in_weight.astype(bf16), "shard", axis=0, tiled=True),
        lax.all_gather(down_weight.astype(bf16), "shard", axis=0, tiled=True),
        lax.all_gather(qk_bias.astype(bf16), "shard", axis=0, tiled=True),
        lax.all_gather(value_bias.astype(bf16), "shard", axis=0, tiled=True),
        lax.all_gather(out_bias.astype(bf16), "shard", axis=0, tiled=True),
        lax.all_gather(in_bias.astype(bf16), "shard", axis=0, tiled=True),
        lax.all_gather(down_bias.astype(bf16), "shard", axis=0, tiled=True),
        lax.all_gather(gain_one.astype(bf16), "shard", axis=0, tiled=True),
        lax.all_gather(shift_one.astype(bf16), "shard", axis=0, tiled=True),
        lax.all_gather(gain_two.astype(bf16), "shard", axis=0, tiled=True),
        lax.all_gather(shift_two.astype(bf16), "shard", axis=0, tiled=True),
    )
    row_count, model_width = block_in.shape
    head_count = model_width // HEAD_DIM
    groups = lax.axis_size("shard")
    length = row_count * groups
    window = min(512, length)
    member = lax.axis_index("shard")
    first_row = member * row_count
    last_end = first_row + row_count
    positions = first_row + jnp.arange(row_count, dtype=jnp.int32)
    query_block = positions // BLOCK
    score_scale = HEAD_DIM ** (-0.5)
    needed = (last_end + window - 1) // window
    inputs = block_in.astype(f32)
    normed, norm_back = jax.vjp(layer_norm, inputs, g_one.astype(f32), s_one.astype(f32))
    normed_low = normed.astype(bf16)
    joint_bias = jnp.concatenate([b_qk.astype(f32), b_value.astype(f32)])
    projected = jnp.dot(normed_low, w_qkv, preferred_element_type=f32) + joint_bias
    queries = rotate(projected[:, :model_width], positions).astype(bf16)
    key_rows = rotate(projected[:, model_width : 2 * model_width], positions).astype(bf16)
    values = projected[:, 2 * model_width :].astype(bf16)
    query_heads = queries.reshape(row_count, head_count, HEAD_DIM)

    def masked_scores(key_piece, key_start):
        piece_rows = key_piece.shape[0]
        key_heads = key_piece.reshape(piece_rows, head_count, HEAD_DIM)
        scores = (
            jnp.einsum("qhd,khd->hqk", query_heads, key_heads, preferred_element_type=f32)
            * score_scale
        )
        key_block = (key_start + jnp.arange(piece_rows, dtype=jnp.int32)) // BLOCK
        allowed = key_block[None, :] <= query_block[:, None]
        return (scores, allowed)

    def absorb(running, key_piece, value_piece, key_start):
        highest, denominator, summed = running
        scores, allowed = masked_scores(key_piece, key_start)
        scores = jnp.where(allowed[None], scores, NEG)
        new_high = jnp.maximum(highest, jnp.max(scores, axis=-1))
        rescale = jnp.exp(highest - new_high)
        weights = jnp.where(allowed[None], jnp.exp(scores - new_high[..., None]), 0.0)
        value_heads = value_piece.reshape(-1, head_count, HEAD_DIM)
        summed = summed * rescale[..., None] + jnp.einsum(
            "hqk,khd->hqd", weights.astype(bf16), value_heads, preferred_element_type=f32
        )
        return (new_high, denominator * rescale + jnp.sum(weights, axis=-1), summed)

    start_state = (
        jnp.full((head_count, row_count), NEG, f32),
        jnp.zeros((head_count, row_count), f32),
        jnp.zeros((head_count, row_count, HEAD_DIM), f32),
    )
    key_piece = lax.all_gather(key_rows, "shard", axis=0, tiled=True)
    value_piece = lax.all_gather(values, "shard", axis=0, tiled=True)
    piece_rows = key_piece.shape[0]
    sub_rows = math.gcd(piece_rows, window)
    usable = jnp.clip((last_end + sub_rows - 1) // sub_rows, 0, piece_rows // sub_rows)

    def advance(block_step, state_inner):
        offset = block_step * sub_rows
        return absorb(
            state_inner,
            lax.dynamic_slice_in_dim(key_piece, offset, sub_rows, 0),
            lax.dynamic_slice_in_dim(value_piece, offset, sub_rows, 0),
            offset,
        )

    highest, denominator, summed = lax.fori_loop(0, usable, advance, start_state)
    attended = summed / denominator[..., None]
    log_norm = highest + jnp.log(denominator)
    mixed = jnp.transpose(attended, (1, 0, 2)).reshape(row_count, model_width).astype(bf16)
    branch = jnp.dot(mixed, w_out, preferred_element_type=f32) + b_out.astype(f32)
    middle = inputs + branch
    normed_two, norm_two_back = jax.vjp(layer_norm, middle, g_two.astype(f32), s_two.astype(f32))
    normed_two_low = normed_two.astype(bf16)
    hidden = jnp.dot(normed_two_low, w_in, preferred_element_type=f32) + b_in.astype(f32)
    active_full, gelu_back = jax.vjp(partial(jax.nn.gelu, approximate=True), hidden)
    active = active_full.astype(bf16)
    result = middle + jnp.dot(active, w_down, preferred_element_type=f32) + b_down.astype(f32)
    stacked = earlier.astype(f32)
    layer_out = depth_weights[4] * result
    for level in range(4):
        layer_out = layer_out + depth_weights[level] * stacked[level]
    grad_earlier = depth_weights[:4][:, None, None] * cotangent[None]
    local_depth = jnp.concatenate(
        [jnp.sum(stacked * cotangent[None], axis=(1, 2)), jnp.sum(result * cotangent)[None]]
    )
    grad_depth = lax.psum(local_depth, ("rep", "shard"))
    grad_result = depth_weights[4] * cotangent
    down_grad = grad_result.astype(bf16)
    grad_down_w = jnp.einsum("tf,td->fd", active, down_grad, preferred_element_type=f32)
    grad_down_b = jnp.sum(down_grad.astype(f32), axis=0)
    grad_active = jnp.einsum("td,fd->tf", down_grad, w_down, preferred_element_type=f32)
    grad_hidden = gelu_back(grad_active)[0].astype(bf16)
    grad_in_w = jnp.einsum("td,tf->df", normed_two_low, grad_hidden, preferred_element_type=f32)
    grad_in_b = jnp.sum(grad_hidden.astype(f32), axis=0)
    grad_normed_two = jnp.einsum("tf,df->td", grad_hidden, w_in, preferred_element_type=f32)
    grad_mid_norm, grad_gain_two, grad_shift_two = norm_two_back(grad_normed_two)
    grad_middle = grad_result + grad_mid_norm
    branch_grad = grad_middle.astype(bf16)
    grad_out_w = jnp.einsum("td,te->de", mixed, branch_grad, preferred_element_type=f32)
    grad_out_b = jnp.sum(branch_grad.astype(f32), axis=0)
    grad_mixed = jnp.einsum("te,de->td", branch_grad, w_out, preferred_element_type=f32).astype(
        bf16
    )
    key_all, value_all = (
        lax.all_gather(key_rows, "shard", axis=0, tiled=True),
        lax.all_gather(values, "shard", axis=0, tiled=True),
    )
    grad_heads = grad_mixed.reshape(row_count, head_count, HEAD_DIM)
    delta = jnp.einsum("qhd,hqd->hq", grad_heads.astype(f32), attended)

    def score_grads(key_piece, value_piece, offset, piece_rows):
        scores, allowed = masked_scores(key_piece, offset)
        probs = jnp.where(allowed[None], jnp.exp(scores - log_norm[..., None]), 0.0)
        value_heads = value_piece.reshape(piece_rows, head_count, HEAD_DIM)
        grad_probs = jnp.einsum("qhd,khd->hqk", grad_heads, value_heads, preferred_element_type=f32)
        grad_scores = (probs * (grad_probs - delta[..., None])).astype(bf16)
        return (probs, grad_scores)

    def retrace(block_step, running):
        grad_query, grad_keys, grad_values = running
        offset = block_step * window
        key_piece = lax.dynamic_slice_in_dim(key_all, offset, window, 0)
        value_piece = lax.dynamic_slice_in_dim(value_all, offset, window, 0)
        probs, grad_scores = score_grads(key_piece, value_piece, offset, window)
        key_heads = key_piece.reshape(window, head_count, HEAD_DIM)
        grad_query = grad_query + jnp.einsum(
            "hqk,khd->qhd", grad_scores, key_heads, preferred_element_type=f32
        )
        piece_keys = (
            jnp.einsum("hqk,qhd->khd", grad_scores, query_heads, preferred_element_type=f32)
            * score_scale
        )
        piece_values = jnp.einsum(
            "hqk,qhd->khd", probs.astype(bf16), grad_heads, preferred_element_type=f32
        )
        grad_keys = lax.dynamic_update_slice_in_dim(
            grad_keys, piece_keys.reshape(window, model_width), offset, 0
        )
        grad_values = lax.dynamic_update_slice_in_dim(
            grad_values, piece_values.reshape(window, model_width), offset, 0
        )
        return (grad_query, grad_keys, grad_values)

    start_back = (
        jnp.zeros((row_count, head_count, HEAD_DIM), f32),
        jnp.zeros((length, model_width), f32),
        jnp.zeros((length, model_width), f32),
    )
    grad_query, grad_keys, grad_values = lax.fori_loop(0, needed, retrace, start_back)
    own_keys, own_values = (
        lax.psum_scatter(
            grad_keys.astype(jnp.bfloat16), "shard", scatter_dimension=0, tiled=True
        ).astype(jnp.float32),
        lax.psum_scatter(
            grad_values.astype(jnp.bfloat16), "shard", scatter_dimension=0, tiled=True
        ).astype(jnp.float32),
    )
    grad_q_turned = rotate(grad_query.reshape(row_count, model_width) * score_scale, -positions)
    grad_k_turned = rotate(own_keys, -positions)
    grad_joint = jnp.concatenate([grad_q_turned, grad_k_turned, own_values], axis=1).astype(bf16)
    grad_qkv_w = jnp.einsum("td,tf->df", normed_low, grad_joint, preferred_element_type=f32)
    joint_sums = jnp.sum(grad_joint.astype(f32), axis=0)
    grad_qk_b = joint_sums[: 2 * model_width]
    grad_value_b = joint_sums[2 * model_width :]
    grad_normed = jnp.einsum("tf,df->td", grad_joint, w_qkv, preferred_element_type=f32)
    grad_in_norm, grad_gain_one, grad_shift_one = norm_back(grad_normed)
    grad_block = grad_middle + grad_in_norm
    (
        own_qkv_w,
        own_out_w,
        own_in_w,
        own_down_w,
        own_qk_b,
        own_value_b,
        own_out_b,
        own_in_b,
        own_down_b,
        own_gain_one,
        own_shift_one,
        own_gain_two,
        own_shift_two,
    ) = (
        lax.psum_scatter(
            grad_qkv_w.astype(jnp.bfloat16), "shard", scatter_dimension=0, tiled=True
        ).astype(jnp.float32),
        lax.psum_scatter(
            grad_out_w.astype(jnp.bfloat16), "shard", scatter_dimension=0, tiled=True
        ).astype(jnp.float32),
        lax.psum_scatter(
            grad_in_w.astype(jnp.bfloat16), "shard", scatter_dimension=0, tiled=True
        ).astype(jnp.float32),
        lax.psum_scatter(
            grad_down_w.astype(jnp.bfloat16), "shard", scatter_dimension=0, tiled=True
        ).astype(jnp.float32),
        lax.psum_scatter(
            grad_qk_b.astype(jnp.bfloat16), "shard", scatter_dimension=0, tiled=True
        ).astype(jnp.float32),
        lax.psum_scatter(
            grad_value_b.astype(jnp.bfloat16), "shard", scatter_dimension=0, tiled=True
        ).astype(jnp.float32),
        lax.psum_scatter(
            grad_out_b.astype(jnp.bfloat16), "shard", scatter_dimension=0, tiled=True
        ).astype(jnp.float32),
        lax.psum_scatter(
            grad_in_b.astype(jnp.bfloat16), "shard", scatter_dimension=0, tiled=True
        ).astype(jnp.float32),
        lax.psum_scatter(
            grad_down_b.astype(jnp.bfloat16), "shard", scatter_dimension=0, tiled=True
        ).astype(jnp.float32),
        lax.psum_scatter(
            grad_gain_one.astype(jnp.bfloat16), "shard", scatter_dimension=0, tiled=True
        ).astype(jnp.float32),
        lax.psum_scatter(
            grad_shift_one.astype(jnp.bfloat16), "shard", scatter_dimension=0, tiled=True
        ).astype(jnp.float32),
        lax.psum_scatter(
            grad_gain_two.astype(jnp.bfloat16), "shard", scatter_dimension=0, tiled=True
        ).astype(jnp.float32),
        lax.psum_scatter(
            grad_shift_two.astype(jnp.bfloat16), "shard", scatter_dimension=0, tiled=True
        ).astype(jnp.float32),
    )
    (
        sum_qkv_w,
        sum_out_w,
        sum_in_w,
        sum_down_w,
        sum_qk_b,
        sum_value_b,
        sum_out_b,
        sum_in_b,
        sum_down_b,
        sum_gain_one,
        sum_shift_one,
        sum_gain_two,
        sum_shift_two,
    ) = (
        lax.psum(own_qkv_w.astype(jnp.bfloat16), "rep").astype(jnp.float32),
        lax.psum(own_out_w.astype(jnp.bfloat16), "rep").astype(jnp.float32),
        lax.psum(own_in_w.astype(jnp.bfloat16), "rep").astype(jnp.float32),
        lax.psum(own_down_w.astype(jnp.bfloat16), "rep").astype(jnp.float32),
        lax.psum(own_qk_b.astype(jnp.bfloat16), "rep").astype(jnp.float32),
        lax.psum(own_value_b.astype(jnp.bfloat16), "rep").astype(jnp.float32),
        lax.psum(own_out_b.astype(jnp.bfloat16), "rep").astype(jnp.float32),
        lax.psum(own_in_b.astype(jnp.bfloat16), "rep").astype(jnp.float32),
        lax.psum(own_down_b.astype(jnp.bfloat16), "rep").astype(jnp.float32),
        lax.psum(own_gain_one.astype(jnp.bfloat16), "rep").astype(jnp.float32),
        lax.psum(own_shift_one.astype(jnp.bfloat16), "rep").astype(jnp.float32),
        lax.psum(own_gain_two.astype(jnp.bfloat16), "rep").astype(jnp.float32),
        lax.psum(own_shift_two.astype(jnp.bfloat16), "rep").astype(jnp.float32),
    )
    return (
        layer_out,
        grad_block,
        grad_earlier,
        sum_qkv_w,
        sum_out_w,
        sum_in_w,
        sum_down_w,
        sum_qk_b,
        sum_value_b,
        sum_out_b,
        sum_in_b,
        sum_down_b,
        sum_gain_one,
        sum_shift_one,
        sum_gain_two,
        sum_shift_two,
        grad_depth,
    )


def solution(mesh):
    placed = (
        P(("rep", "shard"), None),
        P(None, ("rep", "shard"), None),
        P(("rep", "shard"), None),
        P("shard", None),
        P("shard", None),
        P("shard", None),
        P("shard", None),
        P("shard"),
        P("shard"),
        P("shard"),
        P("shard"),
        P("shard"),
        P("shard"),
        P("shard"),
        P("shard"),
        P("shard"),
        P(),
    )
    return jax.shard_map(
        per_device,
        mesh=mesh,
        in_specs=placed,
        out_specs=(
            P(("rep", "shard"), None),
            P(("rep", "shard"), None),
            P(None, ("rep", "shard"), None),
            P("shard", None),
            P("shard", None),
            P("shard", None),
            P("shard", None),
            P("shard"),
            P("shard"),
            P("shard"),
            P("shard"),
            P("shard"),
            P("shard"),
            P("shard"),
            P("shard"),
            P("shard"),
            P(),
        ),
        check_vma=False,
    )
```

profile of v0, /device:TPU:0, one launch (start us, length us, event | category | flops | bytes accessed | tf_op | source)
XLA Modules:
  0.0 1013.6 jit_solution(10046158592452047925)
XLA Ops:
  18.0 31.5 %all-reduce.18 = (bf16[768]{0:T(1024)(128)(2,1)S(1)}, bf16[1536]{0:T(1024)(128)(2,1)S(1)}, bf16[768]{0:T(1024)(128)(2,1)S(1)}, bf16[768]{0:T(1024)(128)(2,1)S(1)...) all-reduce(bf16[768]{0:T(1024)(128)(2,1)S(1)} %dynamic-update-slice, ...), channel_id=1, replica_groups=mesh['rep'=4,'shard'=8] {'shard'}, use_global_device_ids=true, to_apply=%add.3 | all-reduce | flops 6144 | bytes 24576
  50.2 4.9 all-gather.8.cloned.1.call-done
  55.1 4.2 convolution_add_fusion
  63.8 3.7 fusion.79
  69.5 3.3 copy.59
  72.8 2.6 subtract_convert_fusion.2
  77.3 2.3 convert_element_type.271
  83.7 12.8 %all-gather = bf16[8,1,384]{2,1,0:T(2,128)(2,1)S(1)} all-gather(bf16[1,1,384]{2,1,0:T(2,128)(2,1)S(1)} %reshape.419), channel_id=1, replica_groups=mesh['rep'=4,'shard'=8] {'shard'}, dimensions={0}, use_global_device_ids=true | all-gather | bytes 6912 | tf_op jit(solution)/shard_map/all_gather | solution.py:68
  96.6 2.2 fusion.73
  99.9 26.5 %all-gather.12.cloned.1.call-done = bf16[4096,768]{1,0:T(8,128)(2,1)} async-done(((bf16[512,768]{1,0:T(8,128)(2,1)}), bf16[4096,768]{1,0:T(8,128)(2,1)}) %all-gather.12.cloned.1.call-update) | async-done | bytes 6291472 | tf_op jit(solution)/shard_map/all_gather | solution.py:127
  126.4 8.8 copy.60
  135.2 56.8 %all-gather.10.cloned.1.call-done = bf16[4096,768]{0,1:T(8,128)(2,1)} async-done(((bf16[512,768]{0,1:T(8,128)(2,1)}), bf16[4096,768]{0,1:T(8,128)(2,1)}) %all-gather.10.cloned.1.call-update) | async-done | bytes 6291472 | tf_op jit(solution)/shard_map/all_gather | solution.py:126
  193.3 12.1 %while.34 = (s32[]{:T(128)}, f32[12,512]{1,0:T(8,128)S(1)}, f32[12,512]{1,0:T(8,128)S(1)}, f32[12,512,64]{1,2,0:T(8,128)}, s32[]{:T(128)}, /*index=5*/bf16[4096,...) while((s32[]{:T(128)}, f32[12,512]{1,0:T(8,128)S(1)}, ...), condition=%wide.region_5.6_spmd.clone, body=%wide.region_2.5_spmd.clone.sunk | while | flops 847278080 | bytes 60432620 | solution.py:141
  197.4 3.1 fusion.136
  200.6 3.6 multiply_add_fusion.7
  205.3 2.5 fusion.61
  207.9 7.5 all-gather.14.cloned.1.call-done
  215.4 2.4 fusion.82
  219.3 49.7 %all-gather.16.cloned.1.call-done = bf16[768,3072]{1,0:T(8,128)(2,1)} async-done(((bf16[96,3072]{1,0:T(8,128)(2,1)}), bf16[768,3072]{1,0:T(8,128)(2,1)}) %all-gather.16.cloned.1.call-update) | async-done | bytes 4718608 | tf_op jit(solution)/shard_map/all_gather | solution.py:63
  269.0 8.2 fusion.71
  277.1 43.9 %all-gather.18.cloned.1.call-done = bf16[3072,768]{1,0:T(8,128)(2,1)} async-done(((bf16[384,768]{1,0:T(8,128)(2,1)}), bf16[3072,768]{1,0:T(8,128)(2,1)}) %all-gather.18.cloned.1.call-update) | async-done | bytes 4718608 | tf_op jit(solution)/shard_map/all_gather | solution.py:64
  321.0 9.7 fusion.74
  330.8 3.5 multiply_reduce_fusion.2
  341.1 3.5 broadcast.410
  344.6 3.5 broadcast.410.clone
  349.4 38.0 %while.35 = (s32[]{:T(128)}, f32[512,12,64]{0,2,1:T(8,128)}, bf16[4096,768]{0,1:T(8,128)(2,1)}, bf16[4096,768]{0,1:T(8,128)(2,1)}, s32[]{:T(128)}, /*index=5*/bf...) while((s32[]{:T(128)}, f32[512,12,64]{0,2,1:T(8,128)}, ...), condition=%wide.region_11.12_spmd.clone, body=%wide.region_10.11_spmd.clone.sunk | while | flops 2046181376 | bytes 130630112 | solution.py:224
  359.2 3.2 fusion.147
  364.8 5.5 fusion.148
  370.3 4.6 convolution_multiply_fusion.2
  374.9 4.5 fusion.149
  379.4 2.8 constant_dynamic-update-slice_fusion.3
  382.2 4.1 bitcast_add_fusion.2
  390.7 6.4 convolution_convert_fusion.1
  398.3 8.6 convolution_convert_fusion
  408.5 257.7 %reduce-scatter.7.cloned.1.call-done = bf16[512,768]{0,1:T(8,128)(2,1)} async-done(((bf16[4096,768]{0,1:T(8,128)(2,1)}), bf16[512,768]{0,1:T(8,128)(2,1)}) %reduce-scatter.7.cloned.1.call-update) | async-done | bytes 786448 | tf_op jit(solution)/shard_map/reduce_scatter | solution.py:226
  668.3 68.4 %reduce-scatter.9.cloned.1.call-done = bf16[512,768]{0,1:T(8,128)(2,1)} async-done(((bf16[4096,768]{0,1:T(8,128)(2,1)}), bf16[512,768]{0,1:T(8,128)(2,1)}) %reduce-scatter.9.cloned.1.call-update) | async-done | bytes 786448 | tf_op jit(solution)/shard_map/reduce_scatter | solution.py:229
  736.7 5.3 convolution_convert_fusion.2
  744.0 5.2 convert_element_type.278
  749.4 6.1 multiply_reduce_fusion
  755.9 2.3 fusion.72
  760.3 26.4 %all-reduce.17 = (bf16[768]{0:T(1024)(128)(2,1)S(1)}, bf16[1536]{0:T(1024)(128)(2,1)S(1)}, bf16[768]{0:T(1024)(128)(2,1)S(1)}, bf16[768]{0:T(1024)(128)(2,1)S(1)...) all-reduce(bf16[768]{0:T(1024)(128)(2,1)S(1)} %dynamic-update-slice, ...), channel_id=1, replica_groups=mesh['rep'=4,'shard'=8] {'shard'}, use_global_device_ids=true, to_apply=%add.7 | all-reduce | flops 10752 | bytes 43008
  786.7 39.5 %reduce-scatter.15.cloned.1.call-done = bf16[96,3072]{1,0:T(8,128)(2,1)} async-done(((bf16[768,3072]{1,0:T(8,128)(2,1)}), bf16[96,3072]{1,0:T(8,128)(2,1)}) %reduce-scatter.15.cloned.1.call-update) | async-done | bytes 589840 | tf_op jit(solution)/shard_map/reduce_scatter | solution.py:264
  826.2 55.4 %reduce-scatter.17.cloned.1.call-done = bf16[384,768]{1,0:T(8,128)(2,1)} async-done(((bf16[3072,768]{1,0:T(8,128)(2,1)}), bf16[384,768]{1,0:T(8,128)(2,1)}) %reduce-scatter.17.cloned.1.call-update) | async-done | bytes 589840 | tf_op jit(solution)/shard_map/reduce_scatter | solution.py:267
  881.7 44.4 %reduce-scatter.11.cloned.1.call-done = bf16[96,2304]{1,0:T(8,128)(2,1)} async-done(((bf16[768,2304]{1,0:T(8,128)(2,1)}), bf16[96,2304]{1,0:T(8,128)(2,1)}) %reduce-scatter.11.cloned.1.call-update) | async-done | bytes 442384 | tf_op jit(solution)/shard_map/reduce_scatter | solution.py:258
  926.1 15.9 %fusion.53 = (f32[512,768]{1,0:T(8,128)}, f32[512,768]{1,0:T(8,128)S(1)}) fusion(f32[4,512,768]{2,1,0:T(8,128)} %convert_element_type.278, f32[]{:T(128)} %bitcast.16, f32[]{:T(128)} %bitcast.14, f32[]{:T(128)} %bitcast.12, f32[]{:T(128)} %bitcast.10, f32[]{:T(128)} %bitcast.1, f32[768]{0:T(1024)S(1)} %convert_element_type.277, f32[512,768]{1,0:T(8,128)} %copy-done.17, ...), kind=kOutput, calls=%fused_computation.104 | convolution fusion | flops 2435973120 | bytes 22035476 | tf_op jit(solution)/shard_map/dot_general | solution.py:152
  942.0 3.3 multiply_reduce_fusion.1
  946.8 37.9 %psum.111 = f32[5]{0:T(128)} all-reduce(f32[5]{0:T(128)S(1)} %pad_maximum_fusion.5), channel_id=1, replica_groups=mesh['rep'=4,'shard'=8] {'rep','shard'}, use_global_device_ids=true, to_apply=%region_52.53 | all-reduce | flops 5 | bytes 40 | tf_op jit(solution)/shard_map/psum | solution.py:161
  985.3 10.5 %all-reduce.19 = (bf16[192]{0:T(256)(128)(2,1)S(1)}, bf16[96]{0:T(256)(128)(2,1)S(1)}, bf16[96]{0:T(256)(128)(2,1)S(1)}, bf16[384]{0:T(512)(128)(2,1)S(1)}, bf16...) all-reduce(bf16[192]{0:T(256)(128)(2,1)S(1)} %dynamic-slice.9, ...), channel_id=1, replica_groups=mesh['rep'=4,'shard'=8] {'rep'}, use_global_device_ids=true, to_apply=%region_26.27 | all-reduce | flops 1248 | bytes 4992 | tf_op jit(solution)/shard_map/psum | solution.py:317
  (273 shorter events, 67.9 us)
Async XLA Ops:
  7.2 42.4 %copy-start.15 = (bf16[512,768]{1,0:T(8,128)(2,1)S(1)}, bf16[512,768]{1,0:T(8,128)(2,1)}, u32[]{:S(2)}) copy-start(bf16[512,768]{1,0:T(8,128)(2,1)} %param.21) | copy-start | bytes 2359300
  7.2 47.9 %all-gather.8.cloned.1.call-start = ((), (), s32[]{:S(2)}) async-start(), calls=%async_computation.6 | async-start | bytes 3981312 | tf_op jit(solution)/shard_map/all_gather | solution.py:61
  9.3 117.1 %all-gather.12.cloned.1.call-start = ((), (), s32[]{:S(2)}) async-start(), calls=%async_computation.8 | async-start | bytes 7077888 | tf_op jit(solution)/shard_map/all_gather | solution.py:127
  49.6 9.7 copy-start.38
  49.6 9.7 copy-start.54
  49.8 9.5 copy-start.40
  50.1 9.2 copy-start.43
  50.2 9.2 copy-start.49
  62.5 129.4 %all-gather.10.cloned.1.call-start = ((), (), s32[]{:S(2)}) async-start(), calls=%async_computation.7 | async-start | bytes 7077888 | tf_op jit(solution)/shard_map/all_gather | solution.py:126
  76.4 139.0 %all-gather.14.cloned.1.call-start = ((), (), s32[]{:S(2)}) async-start(), calls=%async_computation.9 | async-start | bytes 1327104 | tf_op jit(solution)/shard_map/all_gather | solution.py:62
  77.2 5.9 copy-start.45
  77.2 6.5 copy-start.58
  77.2 19.4 %copy-start.8 = (f32[512,768]{1,0:T(8,128)S(1)}, f32[512,768]{1,0:T(8,128)}, u32[]{:S(2)}) copy-start(f32[512,768]{1,0:T(8,128)} %param.23) | copy-start | bytes 4718596
  77.2 191.8 %all-gather.16.cloned.1.call-start = ((), (), s32[]{:S(2)}) async-start(), calls=%async_computation.10 | async-start | bytes 5308416 | tf_op jit(solution)/shard_map/all_gather | solution.py:63
  79.5 241.5 %all-gather.18.cloned.1.call-start = ((), (), s32[]{:S(2)}) async-start(), calls=%async_computation.11 | async-start | bytes 5308416 | tf_op jit(solution)/shard_map/all_gather | solution.py:64
  81.9 584.3 %reduce-scatter.7.cloned.1.call-start = ((), (), s32[]{:S(2)}) async-start(), calls=%async_computation.12 | async-start | bytes 7077888 | tf_op jit(solution)/shard_map/reduce_scatter | solution.py:226
  205.3 10.1 copy-start.57
  215.4 53.6 %copy-start.56 = (f32[768]{0:T(1024)S(1)}, f32[768]{0:T(1024)}, u32[]{:S(2)}) copy-start(f32[768]{0:T(1024)} %convert_element_type.269) | copy-start | bytes 9220
  219.3 101.7 %copy-start.29 = (bf16[512,768]{1,0:T(8,128)(2,1)S(1)}, bf16[512,768]{1,0:T(8,128)(2,1)}, u32[]{:S(2)}) copy-start(bf16[512,768]{1,0:T(8,128)(2,1)} %get-tuple-element.492) | copy-start | bytes 2359300
  321.0 9.8 copy-start.18
  321.0 9.8 copy-start.61
  370.3 4.6 copy-start.2
  382.1 5.3 copy-start.4
  382.2 5.3 copy-start.24
  387.4 349.3 %reduce-scatter.9.cloned.1.call-start = ((), (), s32[]{:S(2)}) async-start(), calls=%async_computation.13 | async-start | bytes 7077888 | tf_op jit(solution)/shard_map/reduce_scatter | solution.py:229
  388.2 398.5 %reduce-scatter.13.cloned.1.call-start = ((), (), s32[]{:S(2)}) async-start(), calls=%async_computation.15 | async-start | bytes 1327104 | tf_op jit(solution)/shard_map/reduce_scatter | solution.py:261
  390.7 435.5 %reduce-scatter.15.cloned.1.call-start = ((), (), s32[]{:S(2)}) async-start(), calls=%async_computation.16 | async-start | bytes 5308416 | tf_op jit(solution)/shard_map/reduce_scatter | solution.py:264
  397.2 484.5 %reduce-scatter.17.cloned.1.call-start = ((), (), s32[]{:S(2)}) async-start(), calls=%async_computation.17 | async-start | bytes 5308416 | tf_op jit(solution)/shard_map/reduce_scatter | solution.py:267
  406.9 519.1 %reduce-scatter.11.cloned.1.call-start = ((), (), s32[]{:S(2)}) async-start(), calls=%async_computation.14 | async-start | bytes 3981312 | tf_op jit(solution)/shard_map/reduce_scatter | solution.py:258
  408.3 259.2 %copy-start.35 = (f32[512,32]{0,1:T(8,128)S(1)}, f32[512,32]{0,1:T(8,128)}, u32[]{:S(2)}) copy-start(f32[512,32]{0,1:T(8,128)} %get-tuple-element.525) | copy-start | bytes 196612
  408.3 259.3 %copy-start.36 = (f32[512,32]{0,1:T(8,128)S(1)}, f32[512,32]{0,1:T(8,128)}, u32[]{:S(2)}) copy-start(f32[512,32]{0,1:T(8,128)} %get-tuple-element.526) | copy-start | bytes 196612
  668.1 68.6 %copy-start.16 = (bf16[512,768]{1,0:T(8,128)(2,1)S(1)}, bf16[512,768]{1,0:T(8,128)(2,1)}, u32[]{:S(2)}) copy-start(bf16[512,768]{1,0:T(8,128)(2,1)} %param.21) | copy-start | bytes 2359300
  668.1 68.6 %copy-start.39 = (f32[768]{0:T(1024)S(1)}, f32[768]{0:T(1024)}, u32[]{:S(2)}) copy-start(f32[768]{0:T(1024)} %copy-done.38) | copy-start | bytes 9220
  668.1 68.6 %copy-start.41 = (f32[512]{0:T(512)S(1)}, f32[512]{0:T(512)}, u32[]{:S(2)}) copy-start(f32[512]{0:T(512)} %copy-done.40) | copy-start | bytes 6148
  668.1 68.6 %copy-start.50 = (f32[512]{0:T(512)S(1)}, f32[512]{0:T(512)}, u32[]{:S(2)}) copy-start(f32[512]{0:T(512)} %copy-done.49) | copy-start | bytes 6148
  668.1 68.6 %copy-start.55 = (f32[768]{0:T(1024)S(1)}, f32[768]{0:T(1024)}, u32[]{:S(2)}) copy-start(f32[768]{0:T(1024)} %copy-done.54) | copy-start | bytes 9220
  668.2 73.8 %copy-start.25 = (bf16[512,12,64]{0,2,1:T(8,128)(2,1)}, bf16[512,12,64]{0,2,1:T(8,128)(2,1)S(1)}, u32[]{:S(2)}) copy-start(bf16[512,12,64]{0,2,1:T(8,128)(2,1)S(1)} %pad_maximum_fusion.4) | copy-start | bytes 2359300
  742.0 258.5 %all-reduce.23.cloned.1.call-start = ((), (), s32[]{:S(2)}) async-start(), calls=%async_computation.18 | async-start | bytes 3538944 | tf_op jit(solution)/shard_map/psum | solution.py:313
  744.0 5.4 copy-start.9
  744.0 5.4 copy-start.46
  749.4 6.1 copy-start.26
  749.4 6.1 copy-start.32
  749.4 6.5 copy-start.62
  926.1 16.0 %copy-start.14 = (f32[512,768]{1,0:T(8,128)S(1)}, f32[512,768]{1,0:T(8,128)}, u32[]{:S(2)}) copy-start(f32[512,768]{1,0:T(8,128)} %copy-done.13) | copy-start | bytes 4718596
  926.1 16.0 %copy-start.21 = (f32[512,768]{1,0:T(8,128)S(1)}, f32[512,768]{1,0:T(8,128)}, u32[]{:S(2)}) copy-start(f32[512,768]{1,0:T(8,128)} %copy-done.20) | copy-start | bytes 4718596
  926.1 16.0 %copy-start.48 = (f32[512]{0:T(512)S(1)}, f32[512]{0:T(512)}, u32[]{:S(2)}) copy-start(f32[512]{0:T(512)} %copy-done.47) | copy-start | bytes 6148
  1000.5 4.4 copy-start.33
  1000.5 5.4 copy-start.37
  (32 other events, 64.3 us)
Sparse Core Ops, SparseCore 0:
  10.2 44.8 all-gather.7
  62.6 63.7 all-gather.11
  128.6 63.3 all-gather.9
  194.0 21.3 all-gather.13
  217.5 51.4 all-gather.15
  270.5 50.5 all-gather.17
  387.6 278.5 reduce-scatter.6
  668.5 68.1 reduce-scatter.8
  739.6 31.0 reduce-scatter.12
  772.8 53.3 reduce-scatter.14
  828.5 53.0 reduce-scatter.16
  883.8 42.1 reduce-scatter.10
  929.9 64.0 all-reduce.22
where the time goes:
time: 1020 us; the launch traced here: 1010 us
  waiting for transfers between devices  656 us (64%)
  blocking collectives  119 us (12%)
  matrix products  97.6 us (10%)
  other arithmetic  60.4 us (6%)
  local copies, waits for them, and re-layouts  53 us (5%)
  between operations  18.4 us (2%)
    reduce_scatter x1, waiting for transfers between devices, per_device(): lax.psum_scatter(grad_keys.astype(jnp.bfloat16), 'shard', scatter_dimensi...  258 us
    reduce_scatter x1, waiting for transfers between devices, per_device(): lax.psum_scatter(grad_values.astype(jnp.bfloat16), 'shard', scatter_dimen...  68.4 us
    unnamed x2, blocking collectives  57.9 us
    all_gather x1, waiting for transfers between devices, per_device(): key_piece = lax.all_gather(key_rows, 'shard', axis=0, tiled=True)  56.8 us
    reduce_scatter x1, waiting for transfers between devices, per_device(): lax.psum_scatter(grad_down_w.astype(jnp.bfloat16), 'shard', scatter_dimen...  55.4 us
    all_gather x1, waiting for transfers between devices, per_device(): lax.all_gather(in_weight.astype(bf16), 'shard', axis=0, tiled=True)  49.7 us
    reduce_scatter x1, waiting for transfers between devices, per_device(): lax.psum_scatter(grad_qkv_w.astype(jnp.bfloat16), 'shard', scatter_dimens...  44.4 us
    all_gather x1, waiting for transfers between devices, per_device(): lax.all_gather(down_weight.astype(bf16), 'shard', axis=0, tiled=True)  43.9 us
  transfers between devices with their start and end apart: 13, of which 11 were waited for; matrix products, arithmetic and copies ran while one was open for 13% of the time, Pallas kernels for 0%

commit v1 on v0

--- a/solution.py
+++ b/solution.py
@@ -4,6 +4,8 @@
 import jax
 import jax.numpy as jnp
 from jax import lax
+from jax.experimental import pallas as pl
+from jax.experimental.pallas import tpu as pltpu
 from jax.sharding import PartitionSpec as P
 
 HEAD_DIM = 64
@@ -36,7 +38,7 @@
     return turned.reshape(row_count, -1)
 
 
-def per_device(
+def generic_device(
     block_in,
     earlier,
     cotangent,
@@ -345,6 +347,469 @@
     )
 
 
+F32 = jnp.float32
+BF16 = jnp.bfloat16
+CHUNK = 2 * BLOCK
+VMEM_LIMIT = 56 * 1024 * 1024
+
+
+def contract(left, right, left_dim, right_dim):
+    return lax.dot_general(
+        left, right, (((left_dim,), (right_dim,)), ((), ())), preferred_element_type=F32
+    )
+
+
+def qkv_kernel(
+    x_ref, weight_ref, bias_ref, gain_ref, shift_ref, cos_ref, sin_ref,
+    normed_ref, qt_ref, kt_ref, vt_ref, k_ref, v_ref,
+):
+    x = x_ref[...].astype(F32)
+    center = x - jnp.mean(x, axis=-1, keepdims=True)
+    spread = jnp.mean(center * center, axis=-1, keepdims=True)
+    normed = center * lax.rsqrt(spread + EPSILON) * gain_ref[...] + shift_ref[...]
+    low = normed.astype(BF16)
+    normed_ref[...] = low
+    width = qt_ref.shape[0]
+    half = HEAD_DIM // 2
+    joint = contract(weight_ref[...], low, 1, 1) + bias_ref[...]
+    cosine = cos_ref[...]
+    sine = sin_ref[...]
+    for head in range(width // HEAD_DIM):
+        base = head * HEAD_DIM
+        for part in range(2):
+            start = part * width + base
+            former = joint[start : start + half]
+            latter = joint[start + half : start + HEAD_DIM]
+            turned = jnp.concatenate(
+                [former * cosine - latter * sine, former * sine + latter * cosine], axis=0
+            )
+            if part == 0:
+                qt_ref[base : base + HEAD_DIM, :] = (turned * HEAD_DIM ** (-0.5)).astype(BF16)
+            else:
+                kt_ref[base : base + HEAD_DIM, :] = turned.astype(BF16)
+                k_ref[head] = jnp.transpose(turned).astype(BF16)
+        start = 2 * width + base
+        value = joint[start : start + HEAD_DIM]
+        vt_ref[base : base + HEAD_DIM, :] = value.astype(BF16)
+        v_ref[head] = jnp.transpose(value).astype(BF16)
+
+
+def project(tokens, weight_t, bias, gain, shift, cosine, sine):
+    length, model_width = tokens.shape
+    columns = weight_t.shape[0]
+    width = columns // 3
+    heads = width // HEAD_DIM
+    half = HEAD_DIM // 2
+    tile = CHUNK
+    fixed = lambda i: (0, 0)
+    across = lambda i: (0, i)
+    return pl.pallas_call(
+        qkv_kernel,
+        name="project",
+        grid=(length // tile,),
+        in_specs=[
+            pl.BlockSpec((tile, model_width), lambda i: (i, 0)),
+            pl.BlockSpec((columns, model_width), fixed),
+            pl.BlockSpec((columns, 1), fixed),
+            pl.BlockSpec((1, model_width), fixed),
+            pl.BlockSpec((1, model_width), fixed),
+            pl.BlockSpec((half, tile), across),
+            pl.BlockSpec((half, tile), across),
+        ],
+        out_specs=[
+            pl.BlockSpec((tile, model_width), lambda i: (i, 0)),
+            pl.BlockSpec((width, tile), across),
+            pl.BlockSpec((width, tile), across),
+            pl.BlockSpec((width, tile), across),
+            pl.BlockSpec((heads, tile, HEAD_DIM), lambda i: (0, i, 0)),
+            pl.BlockSpec((heads, tile, HEAD_DIM), lambda i: (0, i, 0)),
+        ],
+        out_shape=[
+            jax.ShapeDtypeStruct((length, model_width), BF16),
+            jax.ShapeDtypeStruct((width, length), BF16),
+            jax.ShapeDtypeStruct((width, length), BF16),
+            jax.ShapeDtypeStruct((width, length), BF16),
+            jax.ShapeDtypeStruct((heads, length, HEAD_DIM), BF16),
+            jax.ShapeDtypeStruct((heads, length, HEAD_DIM), BF16),
+        ],
+        compiler_params=pltpu.CompilerParams(vmem_limit_bytes=VMEM_LIMIT),
+    )(tokens, weight_t, bias, gain, shift, cosine, sine)
+
+
+def last_mask(odd):
+    row = lax.broadcasted_iota(jnp.int32, (CHUNK, BLOCK), 0)
+    return row < BLOCK * (1 + odd)
+
+
+def attend_kernel(core_ref, qt_ref, k_ref, vt_ref, low_ref, full_ref, stat_ref):
+    pair = pl.program_id(0)
+    odd = core_ref[0] ^ (pair & 1)
+    width = qt_ref.shape[0]
+    heads = width // HEAD_DIM
+    queries = [qt_ref[h * HEAD_DIM : (h + 1) * HEAD_DIM, :] for h in range(heads)]
+
+    def absorb(step, state, masked):
+        offset = pl.multiple_of(step * CHUNK, CHUNK)
+        fresh = []
+        for h in range(heads):
+            highest, total, summed = state[h]
+            scores = contract(k_ref[h, pl.ds(offset, CHUNK), :], queries[h], 1, 0)
+            if masked:
+                scores = jnp.where(last_mask(odd), scores, NEG)
+            new_high = jnp.maximum(highest, jnp.max(scores, axis=0, keepdims=True))
+            rescale = jnp.exp(highest - new_high)
+            weights = jnp.exp(scores - new_high)
+            total = total * rescale + jnp.sum(weights, axis=0, keepdims=True)
+            values = vt_ref[h * HEAD_DIM : (h + 1) * HEAD_DIM, pl.ds(offset, CHUNK)]
+            summed = summed * rescale + contract(values, weights.astype(BF16), 1, 0)
+            fresh.append((new_high, total, summed))
+        return fresh
+
+    state = [
+        (
+            jnp.full((1, BLOCK), NEG, F32),
+            jnp.zeros((1, BLOCK), F32),
+            jnp.zeros((HEAD_DIM, BLOCK), F32),
+        )
+        for _ in range(heads)
+    ]
+    state = lax.fori_loop(0, pair, lambda i, s: absorb(i, s, False), state)
+    state = absorb(pair, state, True)
+    for h in range(heads):
+        highest, total, summed = state[h]
+        attended = summed / total
+        full_ref[0, h * HEAD_DIM : (h + 1) * HEAD_DIM, :] = attended
+        low_ref[0, h * HEAD_DIM : (h + 1) * HEAD_DIM, :] = attended.astype(BF16)
+        stat_ref[0, h : h + 1, :] = highest + jnp.log(total)
+
+
+def attend(core, qt, k, vt):
+    width, length = qt.shape
+    pairs = length // CHUNK
+    own = lambda j, core: (0, 2 * j + (core[0] ^ (j & 1)))
+    slot = lambda j, core: (j, 0, 0)
+    return pl.pallas_call(
+        attend_kernel,
+        name="attend",
+        grid_spec=pltpu.PrefetchScalarGridSpec(
+            num_scalar_prefetch=1,
+            grid=(pairs,),
+            in_specs=[
+                pl.BlockSpec((width, BLOCK), own),
+                pl.BlockSpec(k.shape, lambda j, core: (0, 0, 0)),
+                pl.BlockSpec(vt.shape, lambda j, core: (0, 0)),
+            ],
+            out_specs=[
+                pl.BlockSpec((1, width, BLOCK), slot),
+                pl.BlockSpec((1, width, BLOCK), slot),
+                pl.BlockSpec((1, 8, BLOCK), slot),
+            ],
+        ),
+        out_shape=[
+            jax.ShapeDtypeStruct((pairs, width, BLOCK), BF16),
+            jax.ShapeDtypeStruct((pairs, width, BLOCK), F32),
+            jax.ShapeDtypeStruct((pairs, 8, BLOCK), F32),
+        ],
+        compiler_params=pltpu.CompilerParams(vmem_limit_bytes=VMEM_LIMIT),
+    )(core, qt, k, vt)
+
+
+def retrace_kernel(
+    core_ref, qt_ref, grad_ref, full_ref, stat_ref, cos_ref, sin_ref, k_ref, v_ref, kt_ref,
+    joint_ref, dk_ref, dv_ref,
+):
+    step_id = pl.program_id(0)
+    pair = pl.num_programs(0) - 1 - step_id
+    odd = core_ref[0] ^ (pair & 1)
+    width = qt_ref.shape[0]
+    heads = width // HEAD_DIM
+    half = HEAD_DIM // 2
+
+    @pl.when(step_id == 0)
+    def _():
+        dk_ref[...] = jnp.zeros_like(dk_ref)
+        dv_ref[...] = jnp.zeros_like(dv_ref)
+
+    queries, grads, deltas, norms = [], [], [], []
+    for h in range(heads):
+        rows = slice(h * HEAD_DIM, (h + 1) * HEAD_DIM)
+        queries.append(qt_ref[rows, :])
+        grad = grad_ref[0, rows, :]
+        grads.append(grad)
+        deltas.append(jnp.sum(grad.astype(F32) * full_ref[0, rows, :], axis=0, keepdims=True))
+        norms.append(stat_ref[0, h : h + 1, :])
+
+    def absorb(step, state, masked):
+        offset = pl.multiple_of(step * CHUNK, CHUNK)
+        keys = pl.ds(offset, CHUNK)
+        fresh = []
+        for h in range(heads):
+            scores = contract(k_ref[h, keys, :], queries[h], 1, 0)
+            probs = jnp.exp(scores - norms[h])
+            if masked:
+                probs = jnp.where(last_mask(odd), probs, 0.0)
+            grad_probs = contract(v_ref[h, keys, :], grads[h], 1, 0)
+            grad_scores = (probs * (grad_probs - deltas[h])).astype(BF16)
+            dv_ref[h, keys, :] += contract(probs.astype(BF16), grads[h], 1, 1)
+            dk_ref[h, keys, :] += contract(grad_scores, queries[h], 1, 1)
+            turned = kt_ref[h * HEAD_DIM : (h + 1) * HEAD_DIM, keys]
+            fresh.append(state[h] + contract(turned, grad_scores, 1, 0))
+        return fresh
+
+    state = [jnp.zeros((HEAD_DIM, BLOCK), F32) for _ in range(heads)]
+    state = lax.fori_loop(0, pair, lambda i, s: absorb(i, s, False), state)
+    state = absorb(pair, state, True)
+    offset = pl.multiple_of(pair * CHUNK, CHUNK)
+    cosine = cos_ref[...]
+    sine = sin_ref[...]
+    for h in range(heads):
+        base = h * HEAD_DIM
+        doubled = jnp.concatenate([state[h], state[h]], axis=1) * HEAD_DIM ** (-0.5)
+        column = lax.broadcasted_iota(jnp.int32, doubled.shape, 1) // BLOCK
+        doubled = jnp.where(column == odd, doubled, 0.0)
+        key_grad = jnp.transpose(dk_ref[h, pl.ds(offset, CHUNK), :])
+        for part, value in ((0, doubled), (1, key_grad)):
+            former = value[:half]
+            latter = value[half:]
+            turned = jnp.concatenate(
+                [former * cosine + latter * sine, latter * cosine - former * sine], axis=0
+            )
+            start = part * width + base
+            joint_ref[start : start + HEAD_DIM, :] = turned.astype(BF16)
+        start = 2 * width + base
+        joint_ref[start : start + HEAD_DIM, :] = jnp.transpose(
+            dv_ref[h, pl.ds(offset, CHUNK), :]
+        ).astype(BF16)
+
+
+def retrace(core, qt, grads, full, stats, cosine, sine, k, v, kt):
+    width, length = qt.shape
+    heads = width // HEAD_DIM
+    half = HEAD_DIM // 2
+    pairs = length // CHUNK
+    back = lambda j: pairs - 1 - j
+    own = lambda j, core: (0, 2 * back(j) + (core[0] ^ (back(j) & 1)))
+    slot = lambda j, core: (back(j), 0, 0)
+    across = lambda j, core: (0, back(j))
+    return pl.pallas_call(
+        retrace_kernel,
+        name="retrace",
+        grid_spec=pltpu.PrefetchScalarGridSpec(
+            num_scalar_prefetch=1,
+            grid=(pairs,),
+            in_specs=[
+                pl.BlockSpec((width, BLOCK), own),
+                pl.BlockSpec((1, width, BLOCK), slot),
+                pl.BlockSpec((1, width, BLOCK), slot),
+                pl.BlockSpec((1, 8, BLOCK), slot),
+                pl.BlockSpec((half, CHUNK), across),
+                pl.BlockSpec((half, CHUNK), across),
+                pl.BlockSpec(k.shape, lambda j, core: (0, 0, 0)),
+                pl.BlockSpec(v.shape, lambda j, core: (0, 0, 0)),
+                pl.BlockSpec(kt.shape, lambda j, core: (0, 0)),
+            ],
+            out_specs=pl.BlockSpec((3 * width, CHUNK), across),
+            scratch_shapes=[
+                pltpu.VMEM((heads, length, HEAD_DIM), F32),
+                pltpu.VMEM((heads, length, HEAD_DIM), F32),
+            ],
+        ),
+        out_shape=jax.ShapeDtypeStruct((3 * width, length), BF16),
+        compiler_params=pltpu.CompilerParams(vmem_limit_bytes=VMEM_LIMIT),
+    )(core, qt, grads, full, stats, cosine, sine, k, v, kt)
+
+
+def head_split_device(
+    block_in,
+    earlier,
+    cotangent,
+    qkv_weight,
+    out_weight,
+    in_weight,
+    down_weight,
+    qk_bias,
+    value_bias,
+    out_bias,
+    in_bias,
+    down_bias,
+    gain_one,
+    shift_one,
+    gain_two,
+    shift_two,
+    depth_weights,
+):
+    row_count, model_width = block_in.shape
+    hidden_width = in_weight.shape[1]
+    groups = lax.axis_size("shard")
+    owners = groups // 2
+    width = model_width // owners
+    part = model_width // groups
+    length = row_count * groups
+    half = HEAD_DIM // 2
+    member = lax.axis_index("shard")
+    owner = member // 2
+    core = member % 2
+
+    tokens = lax.all_gather(block_in, "shard", axis=0, tiled=True)
+    pieces = qkv_weight.astype(BF16).reshape(part, 3, owners, width)
+    pieces = jnp.transpose(pieces, (2, 0, 1, 3)).reshape(owners, part, 3 * width)
+    early = jnp.concatenate([qk_bias, value_bias, gain_one, shift_one]).astype(BF16)
+    early = jnp.pad(early, (0, 3 * width - early.shape[0]))
+    early = jnp.broadcast_to(early, (owners, 1, 3 * width))
+    packet = jnp.concatenate([pieces, early], axis=1)
+    packet = jnp.broadcast_to(packet[:, None], (owners, 2) + packet.shape[1:])
+    packet = packet.reshape(groups, part + 1, 3 * width)
+    packet = lax.all_to_all(packet, "shard", 0, 0)
+    w_own = packet[:, :part].reshape(model_width, 3 * width)
+    early = packet[:, part].astype(F32)
+    b_qk = early[:, : 2 * part].reshape(2 * model_width)
+    b_value = early[:, 2 * part : 3 * part].reshape(model_width)
+    g_one = early[:, 3 * part : 4 * part].reshape(1, model_width)
+    s_one = early[:, 4 * part : 5 * part].reshape(1, model_width)
+    b_joint = jnp.concatenate([b_qk, b_value]).reshape(3, owners, width)
+    b_own = lax.dynamic_index_in_dim(b_joint, owner, 1, keepdims=False).reshape(3 * width, 1)
+
+    freqs = 10000.0 ** (-jnp.arange(half, dtype=F32) / half)
+    angles = freqs[:, None] * jnp.arange(length, dtype=jnp.int32).astype(F32)[None, :]
+    cosine = jnp.cos(angles)
+    sine = jnp.sin(angles)
+    core_index = core.astype(jnp.int32).reshape(1)
+
+    normed_all, qt, kt, vt, k, v = project(
+        tokens, jnp.transpose(w_own), b_own, g_one, s_one, cosine, sine
+    )
+    mixed_own, attended, stats = attend(core_index, qt, k, vt)
+
+    late = jnp.concatenate([out_bias, in_bias, down_bias, gain_two, shift_two]).astype(BF16)
+    late = late.reshape(-1, model_width)
+    late_rows = late.shape[0]
+    gathered = lax.all_gather(
+        jnp.concatenate([out_weight.astype(BF16), late], axis=0), "shard", axis=0
+    )
+    w_out = gathered[:, :part].reshape(model_width, model_width)
+    late = gathered[:, part:].reshape(groups, late_rows * model_width).astype(F32)
+    hidden_part = hidden_width // groups
+    b_out = late[:, :part].reshape(model_width)
+    b_in = late[:, part : part + hidden_part].reshape(hidden_width)
+    b_down = late[:, part + hidden_part : 2 * part + hidden_part].reshape(model_width)
+    g_two = late[:, 2 * part + hidden_part : 3 * part + hidden_part].reshape(model_width)
+    s_two = late[:, 3 * part + hidden_part :].reshape(model_width)
+    w_in = lax.all_gather(in_weight.astype(BF16), "shard", axis=0, tiled=True)
+    w_down = lax.all_gather(down_weight.astype(BF16), "shard", axis=0, tiled=True)
+
+    mixed_two = lax.all_to_all(mixed_own, "shard", 0, 0).reshape(owners, 2, width, BLOCK)
+    first = lax.dynamic_index_in_dim(mixed_two, core, 1, keepdims=False)
+    second = lax.dynamic_index_in_dim(mixed_two, 1 - core, 1, keepdims=False)
+    mixed_t = jnp.concatenate(
+        [first.reshape(model_width, BLOCK), second.reshape(model_width, BLOCK)], axis=1
+    )
+
+    inputs = block_in.astype(F32)
+    branch = contract(mixed_t, w_out, 0, 0) + b_out
+    middle = inputs + branch
+    normed_two, norm_two_back = jax.vjp(layer_norm, middle, g_two, s_two)
+    normed_two_low = normed_two.astype(BF16)
+    hidden = contract(normed_two_low, w_in, 1, 0) + b_in
+    active_full, gelu_back = jax.vjp(partial(jax.nn.gelu, approximate=True), hidden)
+    active = active_full.astype(BF16)
+    result = middle + contract(active, w_down, 1, 0) + b_down
+    stacked = earlier.astype(F32)
+    layer_out = depth_weights[4] * result
+    for level in range(4):
+        layer_out = layer_out + depth_weights[level] * stacked[level]
+    grad_earlier = depth_weights[:4][:, None, None] * cotangent[None]
+    local_depth = jnp.concatenate(
+        [jnp.sum(stacked * cotangent[None], axis=(1, 2)), jnp.sum(result * cotangent)[None]]
+    )
+    grad_result = depth_weights[4] * cotangent
+    down_grad = grad_result.astype(BF16)
+    grad_down_w = contract(active, down_grad, 0, 0)
+    grad_down_b = jnp.sum(down_grad.astype(F32), axis=0)
+    grad_active = contract(down_grad, w_down, 1, 1)
+    grad_hidden = gelu_back(grad_active)[0].astype(BF16)
+    grad_in_w = contract(normed_two_low, grad_hidden, 0, 0)
+    grad_in_b = jnp.sum(grad_hidden.astype(F32), axis=0)
+    grad_normed_two = contract(grad_hidden, w_in, 1, 1)
+    grad_mid_norm, grad_gain_two, grad_shift_two = norm_two_back(grad_normed_two)
+    grad_middle = grad_result + grad_mid_norm
+    branch_grad = grad_middle.astype(BF16)
+    grad_out_w = contract(mixed_t, branch_grad, 1, 0)
+    grad_out_b = jnp.sum(branch_grad.astype(F32), axis=0)
+    grad_mixed_t = contract(w_out, branch_grad, 1, 1).astype(BF16)
+
+    grad_mixed_t = grad_mixed_t.reshape(owners, width, 2, BLOCK)
+    first = lax.dynamic_index_in_dim(grad_mixed_t, core, 2, keepdims=False)
+    second = lax.dynamic_index_in_dim(grad_mixed_t, 1 - core, 2, keepdims=False)
+    grad_own = jnp.stack([first, second], axis=1).reshape(groups, width, BLOCK)
+    grad_own = lax.all_to_all(grad_own, "shard", 0, 0)
+
+    joint_t = retrace(core_index, qt, grad_own, attended, stats, cosine, sine, k, v, kt)
+    grad_normed = contract(joint_t, w_own, 0, 1).astype(BF16)
+    grad_normed = lax.psum_scatter(
+        grad_normed, "shard", scatter_dimension=0, tiled=True
+    ).astype(F32)
+    grad_qkv = contract(normed_all, joint_t, 0, 1).astype(BF16).reshape(groups, part, 3 * width)
+    grad_qkv = lax.all_to_all(grad_qkv, "shard", 0, 0).astype(F32)
+    grad_qkv = jnp.sum(grad_qkv.reshape(owners, 2, part, 3, width), axis=1)
+    grad_qkv = jnp.transpose(grad_qkv, (1, 2, 0, 3)).reshape(part, 3 * model_width)
+    joint_sums = jnp.sum(joint_t.astype(F32), axis=1).reshape(3, width)
+
+    _, norm_back = jax.vjp(layer_norm, inputs, g_one[0], s_one[0])
+    grad_in_norm, grad_gain_one, grad_shift_one = norm_back(grad_normed)
+    grad_block = grad_middle + grad_in_norm
+
+    spread_sums = lax.dynamic_update_slice(
+        jnp.zeros((3, model_width), F32), joint_sums, (0, owner * width)
+    ).reshape(3 * model_width)
+    sizes = (2 * part, part, part, hidden_part, part, part, part, part, part)
+    small = jnp.concatenate(
+        [
+            spread_sums,
+            grad_out_b,
+            grad_in_b,
+            grad_down_b,
+            grad_gain_one,
+            grad_shift_one,
+            grad_gain_two,
+            grad_shift_two,
+            local_depth,
+        ]
+    )
+    small = lax.psum(small, ("rep", "shard"))
+    small_outs = []
+    start = 0
+    for size in sizes:
+        small_outs.append(lax.dynamic_slice_in_dim(small, start + member * size, size, 0))
+        start += size * groups
+    grad_depth = small[start:]
+
+    sums = [
+        lax.psum_scatter(grad.astype(BF16), "shard", scatter_dimension=0, tiled=True)
+        for grad in (grad_out_w, grad_in_w, grad_down_w)
+    ]
+    sums = [
+        lax.psum(grad, "rep").astype(F32) for grad in [grad_qkv.astype(BF16)] + sums
+    ]
+    return (layer_out, grad_block, grad_earlier, *sums, *small_outs, grad_depth)
+
+
+def per_device(*args):
+    block_in = args[0]
+    row_count, model_width = block_in.shape
+    groups = lax.axis_size("shard")
+    head_count = model_width // HEAD_DIM
+    late_size = (4 * model_width + args[5].shape[1]) // groups
+    if (
+        groups % 2 == 0
+        and row_count == CHUNK
+        and head_count % (groups // 2) == 0
+        and head_count // (groups // 2) <= 8
+        and late_size % model_width == 0
+    ):
+        return head_split_device(*args)
+    return generic_device(*args)
+
+
 def solution(mesh):
     placed = (
         P(("rep", "shard"), None),

time: 1020 us -> 627 us (0.61)
  waiting for transfers between devices: 656 us -> 215 us
  Pallas kernels: 0 us -> 110 us
  local copies, waits for them, and re-layouts: 53 us -> 32.2 us
  matrix products: 97.6 us -> 77.3 us
  other arithmetic: 60.4 us -> 43.5 us
    reduce_scatter x6 -> x4, waiting for transfers between devices: 466 us -> 70.6 us  [the longest x1 67.1 us: head_split_device(): lax.psum_scatter(grad_normed, 'shard', scatter_dimension=0, tiled=True)]
    all_gather x6 -> x4, waiting for transfers between devices: 189 us -> 45 us  [the longest x1 29.1 us: head_split_device(): lax.all_gather(down_weight.astype(BF16), 'shard', axis=0, tiled=True)]
    pallas_call x0 -> x3, Pallas kernels: none -> 110 us  [the longest x1 50.4 us: attend(): pl.pallas_call(attend_kernel, name='attend', grid_spec=pltpu.PrefetchScal...]
    all_to_all x0 -> x2, blocking collectives: none -> 77.3 us  [the longest x1 44.6 us: head_split_device(): grad_qkv = lax.all_to_all(grad_qkv, 'shard', 0, 0).astype(F32)]
    all_to_all x0 -> x2, waiting for transfers between devices: none -> 66.3 us  [the longest x1 52.7 us: head_split_device(): packet = lax.all_to_all(packet, 'shard', 0, 0)]
    unnamed x2 -> x0, blocking collectives: 57.9 us -> none
    psum x1, waiting for transfers between devices: 0.01 us -> 31.9 us  [head_split_device(): lax.psum(grad, 'rep').astype(F32)]
    dot_general x19 -> x11, matrix products: 97.6 us -> 77.3 us  [contract(): lax.dot_general(left, right, (((left_dim,), (right_dim,)), ((), ())), pre...]
  transfers between devices with their start and end apart: 13 -> 11, of which waited for: 11 -> 7; matrix products, arithmetic and copies ran while one was open for 13% -> 19% of each run, Pallas kernels for 0% -> 18%
where the time goes in v1:
time: 627 us; the launch traced here: 619 us
  waiting for transfers between devices  215 us (34%)
  blocking collectives  115 us (18%)
  Pallas kernels  110 us (18%)
  matrix products  77.3 us (12%)
  other arithmetic  43.5 us (7%)
  local copies, waits for them, and re-layouts  32.2 us (5%)
  between operations  14.6 us (2%)
  starting transfers between devices  11 us (2%)
    dot_general x11, matrix products, contract(): lax.dot_general(left, right, (((left_dim,), (right_dim,)), ((), ())), pre...  77.3 us
    reduce_scatter x1, waiting for transfers between devices, head_split_device(): lax.psum_scatter(grad_normed, 'shard', scatter_dimension=0, tiled=True)  67.1 us
    all_to_all x1, waiting for transfers between devices, head_split_device(): packet = lax.all_to_all(packet, 'shard', 0, 0)  52.7 us
    pallas_call x1, Pallas kernels, attend(): pl.pallas_call(attend_kernel, name='attend', grid_spec=pltpu.PrefetchScal...  50.4 us
    pallas_call x1, Pallas kernels, retrace(): pl.pallas_call(retrace_kernel, name='retrace', grid_spec=pltpu.PrefetchSc...  45.6 us
    all_to_all x1, blocking collectives, head_split_device(): grad_qkv = lax.all_to_all(grad_qkv, 'shard', 0, 0).astype(F32)  44.6 us
    psum x1, blocking collectives, head_split_device(): small = lax.psum(small, ('rep', 'shard'))  38.1 us
    all_to_all x1, blocking collectives, head_split_device(): grad_own = lax.all_to_all(grad_own, 'shard', 0, 0)  32.7 us
  transfers between devices with their start and end apart: 11, of which 7 were waited for; matrix products, arithmetic and copies ran while one was open for 19% of the time, Pallas kernels for 18%

profile of v1, /device:TPU:0, one launch (start us, length us, event | category | flops | bytes accessed | tf_op | source)
XLA Modules:
  0.0 618.9 jit_solution(9510822010024831451)
XLA Ops:
  8.7 1.1 convert_element_type.129
  16.7 1.1 broadcast_in_dim.17
  17.7 6.3 %all-to-all-start = ((bf16[8,97,576]{2,1,0:T(8,128)(2,1)}), bf16[8,97,576]{2,1,0:T(8,128)(2,1)S(1)}, u32[]{:S(2)}, u32[]{:S(2)}) async-start(bf16[8,97,576]{2,1,0:T(8,128)(2,1)} %bitcast.4), calls=%async_computation | async-start | bytes 2129920 | tf_op jit(solution)/shard_map/all_to_all | solution.py:662
  24.1 2.8 multiply_sine_fusion
  26.9 52.7 %all-to-all-done = bf16[8,97,576]{2,1,0:T(8,128)(2,1)S(1)} async-done(((bf16[8,97,576]{2,1,0:T(8,128)(2,1)}), bf16[8,97,576]{2,1,0:T(8,128)(2,1)S(1)}, u32[]{:S(2)}, u32[]{:S(2)}) %all-to-all-start) | async-done | bytes 893984 | tf_op jit(solution)/shard_map/all_to_all | solution.py:662
  82.4 1.3 copy.63
  83.6 15.9 %all-gather.7.cloned.1.call-done.x_ref = bf16[4096,768]{1,0:T(8,128)(2,1)} async-done(((bf16[512,768]{1,0:T(8,128)(2,1)}), bf16[4096,768]{1,0:T(8,128)(2,1)}) %all-gather.7.cloned.1.call-update) | async-done | bytes 6291472 | tf_op jit(solution)/shard_map/all_gather | solution.py:653
  99.5 14.2 %project.1 = (bf16[4096,768]{1,0:T(8,128)(2,1)}, bf16[192,4096]{1,0:T(8,128)(2,1)}, bf16[192,4096]{1,0:T(8,128)(2,1)}, bf16[192,4096]{1,0:T(8,128)(2,1)}, bf16[3...) custom-call(bf16[4096,768]{1,0:T(8,128)(2,1)} %all-gather.7.cloned.1.call-done.x_ref, bf16[576,768]{1,0:T(8,128)(2,1)} %bitcast.89, ...), custom_call_target="tpu_custom_call" | custom-call | tf_op jit(solution)/shard_map/project/pallas_call | solution.py:406
  113.8 50.4 %attend.1 = (bf16[8,192,256]{2,1,0:T(8,128)(2,1)}, f32[8,192,256]{2,1,0:T(8,128)}, f32[8,8,256]{2,1,0:T(8,128)}) custom-call(s32[1]{0:T(128)} %bitcast.1.core_ref, bf16[192,4096]{1,0:T(8,128)(2,1)} %get-tuple-element.26.qt_ref, bf16[3,4096,64]{2,1,0:T(8,128)(2,1)} %get-tuple-element.27.k_ref, bf16[192,4096]{1,0:T(8,128)(2,1)} %get-tuple-element.28.vt_ref), custom_call_target="tpu_custom_call" | custom-call | tf_op jit(solution)/shard_map/attend/pallas_call | solution.py:491
  164.2 3.7 all-to-all-start.1
  168.8 2.3 convert_reduce_fusion.4
  175.3 2.4 slice.103
  177.7 13.5 %all-to-all-done.1 = bf16[8,192,256]{2,1,0:T(8,128)(2,1)S(1)} async-done(((bf16[8,192,256]{2,1,0:T(8,128)(2,1)}), bf16[8,192,256]{2,1,0:T(8,128)(2,1)S(1)}, u32[]{:S(2)}, u32[]{:S(2)}) %all-to-all-start.1) | async-done | bytes 786464 | tf_op jit(solution)/shard_map/all_to_all | solution.py:700
  191.3 1.3 copy-done.11
  193.6 1.1 copy-done.5
  195.6 8.3 %fusion.36 = f32[512,3072]{1,0:T(8,128)} fusion(bf16[768,3072]{1,0:T(8,128)(2,1)} %all-gather.9.cloned.1.call-done, f32[512,768]{1,0:T(8,128)} %copy-done.5, f32[768]{0:T(1024)} %add.186, f32[768]{0:T(1024)} %mul.272, f32[512]{0:T(512)} %fusion.32, f32[512]{0:T(512)S(1)} %broadcast_multiply_fusion.2), kind=kOutput, calls=%fused_computation.106 | convolution fusion | flops 2417885184 | bytes 12593152 | tf_op jit(solution)/shard_map/dot_general | solution.py:357
  203.9 29.1 %all-gather.11.cloned.1.call-done = bf16[3072,768]{1,0:T(8,128)(2,1)} async-done(((bf16[384,768]{1,0:T(8,128)(2,1)}), bf16[3072,768]{1,0:T(8,128)(2,1)}) %all-gather.11.cloned.1.call-update) | async-done | bytes 4718608 | tf_op jit(solution)/shard_map/all_gather | solution.py:698
  233.1 9.7 %convert_reduce_fusion.1 = (f32[3072]{0:T(1024)}, bf16[512,3072]{1,0:T(8,128)(2,1)S(1)}) fusion(f32[512,3072]{1,0:T(8,128)} %fusion.36, f32[3072]{0:T(1024)} %add.189, bf16[512,768]{1,0:T(8,128)(2,1)S(1)} %copy-done.14, bf16[3072,768]{1,0:T(8,128)(2,1)} %all-gather.11.cloned.1.call-done), kind=kOutput, calls=%fused_computation.12 | convolution fusion | flops 2452091904 | bytes 14966784 | tf_op jit(solution)/shard_map/dot_general | solution.py:357
  242.8 3.5 multiply_reduce_fusion.2
  247.0 1.7 convert_reduce_fusion.5
  249.6 1.8 convolution_convert_fusion.3
  251.7 7.5 %convolution_convert_fusion.2 = bf16[768,3072]{1,0:T(8,128)(2,1)} fusion(bf16[512,3072]{1,0:T(8,128)(2,1)} %copy-done.38, f32[512,768]{1,0:T(8,128)} %copy-done.5, f32[768]{0:T(1024)} %add.186, f32[768]{0:T(1024)} %mul.272, f32[512]{0:T(512)} %fusion.32, f32[512]{0:T(512)S(1)} %broadcast_multiply_fusion.2), kind=kOutput, calls=%fused_computation.15 | convolution fusion | flops 2420244480 | bytes 9447424 | tf_op jit(solution)/shard_map/dot_general | solution.py:357
  259.9 8.7 %convolution_convert_fusion.1 = bf16[3072,768]{1,0:T(8,128)(2,1)} fusion(bf16[512,768]{1,0:T(8,128)(2,1)S(1)} %copy-done.14, f32[512,3072]{1,0:T(8,128)} %fusion.36, f32[3072]{0:T(1024)S(1)} %copy-done.26), kind=kOutput, calls=%fused_computation.14 | convolution fusion | flops 2434007040 | bytes 11808768 | tf_op jit(solution)/shard_map/dot_general | solution.py:357
  268.6 1.2 copy-done.12
  269.8 2.8 convolution_convert_fusion.5
  272.7 2.2 reshape.288
  274.9 1.6 constant_dynamic-slice_fusion.1
  276.8 32.7 %all_to_all.20.grad_ref = bf16[8,192,256]{2,1,0:T(8,128)(2,1)} all-to-all(bf16[8,192,256]{2,1,0:T(8,128)(2,1)S(1)} %bitcast.90), channel_id=1, replica_groups=mesh['rep'=4,'shard'=8] {'shard'}, dimensions={0} | all-to-all | bytes 1572864 | tf_op jit(solution)/shard_map/all_to_all | solution.py:744
  309.5 45.6 %retrace.1 = bf16[576,4096]{1,0:T(8,128)(2,1)} custom-call(s32[1]{0:T(128)} %bitcast.1.core_ref, bf16[192,4096]{1,0:T(8,128)(2,1)} %get-tuple-element.26.qt_ref, bf16[8,192,256]{2,1,0:T(8,128)(2,1)} %all_to_all.20.grad_ref, f32[8,192,256]{2,1,0:T(8,128)} %get-tuple-element.30.full_ref, f32[8,8,256]{2,1,0:T(8,128)} %get-tuple-element.31.stat_ref, ...), custom_call_target="tpu_custom_call" | custom-call | tf_op jit(solution)/shard_map/retrace/pallas_call | solution.py:594
  355.1 8.9 %convolution_convert_fusion.4 = bf16[768,576]{0,1:T(8,128)(2,1)} fusion(bf16[576,4096]{1,0:T(8,128)(2,1)} %retrace.1, bf16[4096,768]{1,0:T(8,128)(2,1)} %get-tuple-element.34), kind=kOutput, calls=%fused_computation.57 | convolution fusion | flops 3624321024 | bytes 11894784 | tf_op jit(solution)/shard_map/dot_general | solution.py:357
  364.0 1.5 copy.68
  365.6 44.6 %all_to_all.21 = bf16[8,96,576]{2,1,0:T(8,128)(2,1)S(1)} all-to-all(bf16[8,96,576]{2,1,0:T(8,128)(2,1)S(1)} %bitcast.88), channel_id=1, replica_groups=mesh['rep'=4,'shard'=8] {'shard'}, dimensions={0} | all-to-all | bytes 1769472 | tf_op jit(solution)/shard_map/all_to_all | solution.py:752
  410.6 1.3 copy.70
  411.9 2.4 convert_element_type.146
  414.4 3.5 reduce-scatter.11.cloned.1.call-done
  418.1 9.5 %convolution_convert_fusion = bf16[4096,768]{1,0:T(8,128)(2,1)} fusion(bf16[576,4096]{1,0:T(8,128)(2,1)} %retrace.1, bf16[768,576]{1,0:T(8,128)(2,1)S(1)} %bitcast.87), kind=kOutput, calls=%fused_computation.3 | convolution fusion | flops 3627024384 | bytes 11894784 | tf_op jit(solution)/shard_map/dot_general | solution.py:357
  427.6 5.0 convert_element_type.136
  432.9 5.9 multiply_reduce_fusion
  439.0 15.7 %fusion.16 = (f32[512,768]{1,0:T(8,128)}, f32[512,768]{1,0:T(8,128)}) fusion(f32[4,512,768]{2,1,0:T(8,128)} %convert_element_type.136, f32[]{:T(128)} %bitcast.22, f32[]{:T(128)} %bitcast.20, f32[]{:T(128)} %bitcast.18, f32[]{:T(128)} %bitcast.16, f32[]{:T(128)} %bitcast, f32[768]{0:T(1024)S(1)} %add.195, f32[512,768]{1,0:T(8,128)} %copy-done.5, ...), kind=kOutput, calls=%fused_computation.35 | convolution fusion | flops 2435973120 | bytes 22035476 | tf_op jit(solution)/shard_map/dot_general | solution.py:357
  454.6 3.1 convert_reduce_fusion
  458.0 31.9 %all-reduce.4.cloned.1.call-done = (bf16[96,2304]{1,0:T(8,128)(2,1)}, bf16[96,768]{1,0:T(8,128)(2,1)}, bf16[96,3072]{1,0:T(8,128)(2,1)}, bf16[384,768]{1,0:T(8,128)(2,1)}) async-done(((bf16[96,2304]{1,0:T(8,128)(2,1)}, bf16[96,768]{1,0:T(8,128)(2,1)}, bf16[96,3072]{1,0:T(8,128)(2,1)}, bf16[384,768]{1,0:T(8,128)(2,1)}), (bf16[96,2304]{1,0:T(8,128)(2,1)}, bf16[96,768]{1,0:T(8,128)(2,1)}, ...) | async-done | bytes 1769488 | tf_op jit(solution)/shard_map/psum | solution.py:791
  489.9 2.3 convert_element_type.151
  492.2 1.1 convert_element_type.153
  495.0 67.1 %reduce-scatter.5.cloned.1.call-done = bf16[512,768]{1,0:T(8,128)(2,1)} async-done(((bf16[4096,768]{1,0:T(8,128)(2,1)}), bf16[512,768]{1,0:T(8,128)(2,1)}) %reduce-scatter.5.cloned.1.call-update) | async-done | bytes 786448 | tf_op jit(solution)/shard_map/reduce_scatter | solution.py:748
  562.1 2.0 fusion.12
  564.1 2.1 fusion.14
  566.2 4.7 multiply_reduce_fusion.1
  571.7 38.1 %psum.39 = f32[9989]{0:T(1024)S(1)} all-reduce(f32[9989]{0:T(1024)S(1)} %concatenate.51), channel_id=1, replica_groups=mesh['rep'=4,'shard'=8] {'rep','shard'}, use_global_device_ids=true, to_apply=%region_27.28 | all-reduce | flops 9989 | bytes 79912 | tf_op jit(solution)/shard_map/psum | solution.py:778
  (171 shorter events, 27.0 us)
Async XLA Ops:
  7.2 4.8 copy-start.9
  7.2 92.4 %all-gather.7.cloned.1.call-start = ((), (), s32[]{:S(2)}) async-start(), calls=%async_computation.8 | async-start | bytes 7077888 | tf_op jit(solution)/shard_map/all_gather | solution.py:653
  7.9 163.1 %all-gather.13.cloned.1.call-start = ((), (), s32[]{:S(2)}) async-start(), calls=%async_computation.15 | async-start | bytes 1437696 | tf_op jit(solution)/shard_map/all_gather | solution.py:686
  8.7 4.3 copy-start.10
  11.9 183.7 %all-gather.9.cloned.1.call-start = ((), (), s32[]{:S(2)}) async-start(), calls=%async_computation.9 | async-start | bytes 5308416 | tf_op jit(solution)/shard_map/all_gather | solution.py:697
  12.9 1.4 copy-start.13
  12.9 220.2 %all-gather.11.cloned.1.call-start = ((), (), s32[]{:S(2)}) async-start(), calls=%async_computation.10 | async-start | bytes 5308416 | tf_op jit(solution)/shard_map/all_gather | solution.py:698
  14.2 1.5 copy-start.34
  14.2 1.5 copy-start.35
  14.2 1.5 copy-start.36
  14.2 1.5 copy-start.37
  17.7 61.9 %all-to-all-start = ((bf16[8,97,576]{2,1,0:T(8,128)(2,1)}), bf16[8,97,576]{2,1,0:T(8,128)(2,1)S(1)}, u32[]{:S(2)}, u32[]{:S(2)}) async-start(bf16[8,97,576]{2,1,0:T(8,128)(2,1)} %bitcast.4), calls=%async_computation | async-start | bytes 2129920 | tf_op jit(solution)/shard_map/all_to_all | solution.py:662
  82.3 31.4 %copy-start.7 = (bf16[8,96,576]{2,1,0:T(8,128)(2,1)}, bf16[8,96,576]{2,1,0:T(8,128)(2,1)S(1)}, u32[]{:S(2)}) copy-start(bf16[8,96,576]{2,1,0:T(8,128)(2,1)S(1)} %slice.97) | copy-start | bytes 2654212
  164.2 4.0 copy-start.21
  164.2 4.6 copy-start
  164.2 27.0 %all-to-all-start.1 = ((bf16[8,192,256]{2,1,0:T(8,128)(2,1)}), bf16[8,192,256]{2,1,0:T(8,128)(2,1)S(1)}, u32[]{:S(2)}, u32[]{:S(2)}) async-start(bf16[8,192,256]{2,1,0:T(8,128)(2,1)} %get-tuple-element.29), calls=%async_computation.1 | async-start | bytes 1572864 | tf_op jit(solution)/shard_map/all_to_all | solution.py:700
  167.9 246.5 %reduce-scatter.7.cloned.1.call-start = ((), (), s32[]{:S(2)}) async-start(), calls=%async_computation.12 | async-start | bytes 1327104 | tf_op jit(solution)/shard_map/reduce_scatter | solution.py:787
  175.3 16.0 %copy-start.1 = (bf16[512,768]{1,0:T(8,128)(2,1)S(1)}, bf16[512,768]{1,0:T(8,128)(2,1)}, u32[]{:S(2)}) copy-start(bf16[512,768]{1,0:T(8,128)(2,1)} %param.17) | copy-start | bytes 2359300
  175.3 16.0 %copy-start.32 = (f32[768]{0:T(1024)S(1)}, f32[768]{0:T(1024)}, u32[]{:S(2)}) copy-start(f32[768]{0:T(1024)} %add.181) | copy-start | bytes 9220
  191.3 1.4 copy-start.11
  191.3 2.3 copy-start.18
  193.6 1.1 copy-start.5
  195.6 37.4 %copy-start.14 = (bf16[512,768]{1,0:T(8,128)(2,1)S(1)}, bf16[512,768]{1,0:T(8,128)(2,1)}, u32[]{:S(2)}) copy-start(bf16[512,768]{1,0:T(8,128)(2,1)} %get-tuple-element.48) | copy-start | bytes 2359300
  233.1 9.7 %copy-start.6 = (f32[512,768]{1,0:T(8,128)S(1)}, f32[512,768]{1,0:T(8,128)}, u32[]{:S(2)}) copy-start(f32[512,768]{1,0:T(8,128)} %copy-done.5) | copy-start | bytes 4718596
  233.1 9.7 %copy-start.25 = (f32[768]{0:T(1024)S(1)}, f32[768]{0:T(1024)}, u32[]{:S(2)}) copy-start(f32[768]{0:T(1024)} %mul.272) | copy-start | bytes 9220
  233.1 9.7 %copy-start.29 = (f32[512]{0:T(512)S(1)}, f32[512]{0:T(512)}, u32[]{:S(2)}) copy-start(f32[512]{0:T(512)} %fusion.32) | copy-start | bytes 6148
  233.1 9.7 %copy-start.33 = (bf16[768,3072]{1,0:T(8,128)(2,1)S(1)}, bf16[768,3072]{1,0:T(8,128)(2,1)}, u32[]{:S(2)}) copy-start(bf16[768,3072]{1,0:T(8,128)(2,1)} %all-gather.9.cloned.1.call-done) | copy-start | bytes 14155780
  242.8 3.5 copy-start.38
  247.0 1.7 copy-start.2
  247.0 2.6 copy-start.19
  251.4 163.0 %reduce-scatter.9.cloned.1.call-start = ((), (), s32[]{:S(2)}) async-start(), calls=%async_computation.13 | async-start | bytes 5308416 | tf_op jit(solution)/shard_map/reduce_scatter | solution.py:787
  259.2 158.7 %reduce-scatter.11.cloned.1.call-start = ((), (), s32[]{:S(2)}) async-start(), calls=%async_computation.14 | async-start | bytes 5308416 | tf_op jit(solution)/shard_map/reduce_scatter | solution.py:787
  268.6 1.3 copy-start.12
  268.6 221.3 %all-reduce.4.cloned.1.call-start = ((), (), s32[]{:S(2)}) async-start(), calls=%async_computation.16 | async-start | bytes 3538944 | tf_op jit(solution)/shard_map/psum | solution.py:791
  411.9 6.2 %copy-start.8 = (bf16[8,96,576]{2,1,0:T(8,128)(2,1)S(1)}, bf16[8,96,576]{2,1,0:T(8,128)(2,1)}, u32[]{:S(2)}) copy-start(bf16[8,96,576]{2,1,0:T(8,128)(2,1)} %copy-done.7) | copy-start | bytes 2654212
  417.9 144.1 %reduce-scatter.5.cloned.1.call-start = ((), (), s32[]{:S(2)}) async-start(), calls=%async_computation.11 | async-start | bytes 7077888 | tf_op jit(solution)/shard_map/reduce_scatter | solution.py:748
  432.9 6.0 copy-start.23
  432.9 6.1 copy-start.27
  489.9 2.3 copy-start.16
  489.9 3.4 copy-start.17
  492.2 2.1 copy-start.20
  562.1 4.1 copy-start.3
  562.1 4.1 copy-start.4
  566.2 4.7 copy-start.22
  566.2 4.7 copy-start.24
  566.2 4.7 copy-start.28
  566.2 4.7 copy-start.30
  566.2 4.7 copy-start.31
  (2 other events, 1.6 us)
Sparse Core Ops, SparseCore 0:
  9.7 89.8 all-gather.6
  101.2 21.8 all-gather.12
  124.7 53.4 all-gather.8
  179.7 53.3 all-gather.10
  251.5 31.6 reduce-scatter.6
  285.4 57.9 reduce-scatter.8
  345.7 72.1 reduce-scatter.10
  421.9 67.9 all-reduce.3
  492.2 69.7 reduce-scatter.4
